TPU v7x, 32 devices: a whole 2x2x4 slice. The times are simulated.
32 devices in a mesh: row: 8 (over z, x), col: 4 (over y, core).
Axes of the slice: x: 2, y: 2, z: 4, core: 2. Of those that a mesh axis runs over, the one named last changes fastest.
Arguments:
- right_side: float32 [6, 8, 64, 128], P(None, 'row'), may hold values from -6 to 6
- inverses: float32 [6, 8, 128, 128], P(None, 'row'), may hold values from -1 to 3
- factor_blocks: bfloat16 [15, 8, 8, 128, 128], P(None, 'row', 'col'), may hold values from -0.15625 to 0.15625
- pattern: int32 [15, 8, 8], P(None, 'row', 'col'), may hold values 0 or 1
Outputs:
- forward_part: float32 [6, 8, 64, 128], P(None, 'row')
- solution: float32 [6, 8, 64, 128], P(None, 'row')
All inputs are finite; a program needn't handle non-finite values. No bound on the sum of `pattern` on one device may be relied on, other than what follows from the above.
Results may differ from a plain program's by a relative error of at most 0.014.
Values may be sent and summed in bfloat16 or wider, within the bound.
No kernel may reach another device: no remote copies, remote signals or barrier semaphores. Data moves between devices by JAX's collectives and lax.ppermute only.
A program may use at most 64 MiB of HBM per device.

v0:
```python
import jax
import jax.numpy as jnp
from jax import lax
from jax.sharding import PartitionSpec as P


def spread(block, axis, holder):
    block = jnp.where(lax.axis_index(axis) == holder, block, jnp.zeros_like(block))
    return lax.psum(block, axis)


def pair_number(higher, lower_level):
    return higher * (higher - 1) // 2 + lower_level


def masked_block(factor_blocks, pattern, pair_index):
    return jnp.where(
        pattern[pair_index][:, :, None, None] != 0,
        factor_blocks[pair_index],
        jnp.zeros((), factor_blocks.dtype),
    )


def shards(right_side, inverses, factor_blocks, pattern):
    levels = right_side.shape[0]
    width_col = factor_blocks.shape[2]
    row_index = lax.axis_index("row")
    col_index = lax.axis_index("col")
    solved = []
    gathered = []
    for height in range(levels):
        remaining = right_side[height]
        if height > 0:
            partial_value = jnp.zeros(remaining.shape, jnp.float32)
            for earlier in range(height):
                masked = masked_block(factor_blocks, pattern, pair_number(height, earlier))
                partial_value = partial_value + jnp.einsum(
                    "ikab,knb->ina", masked, gathered[earlier], preferred_element_type=jnp.float32
                )
            summed = lax.psum(partial_value.astype(jnp.bfloat16), "col").astype(jnp.float32)
            remaining = remaining - summed
        segment = jnp.einsum(
            "inb,iab->ina", remaining, inverses[height], precision=lax.Precision.HIGHEST
        )
        solved.append(segment)
        if height < levels - 1:
            gathered_all = lax.all_gather(segment.astype(jnp.bfloat16), "row", axis=0, tiled=True)
            gathered.append(
                lax.dynamic_slice_in_dim(gathered_all, col_index * width_col, width_col, 0)
            )
    results = [None] * levels
    settled = [None] * levels
    for height in range(levels - 1, -1, -1):
        remaining = solved[height]
        if height < levels - 1:
            partial_value = jnp.zeros((width_col,) + remaining.shape[1:], jnp.float32)
            for later in range(height + 1, levels):
                masked = masked_block(factor_blocks, pattern, pair_number(later, height))
                partial_value = partial_value + jnp.einsum(
                    "ikab,ina->knb", masked, settled[later], preferred_element_type=jnp.float32
                )
            offset = jnp.clip(row_index - col_index * width_col, 0, width_col - 1)
            owner_col = row_index // width_col
            summed = lax.psum(partial_value, "row")
            own_sum = lax.dynamic_slice_in_dim(summed, offset, 1, 0)
            own_sum = spread(own_sum.astype(jnp.bfloat16), "col", owner_col).astype(own_sum.dtype)
            remaining = remaining - own_sum
        segment = jnp.einsum(
            "ina,iab->inb", remaining, inverses[height], precision=lax.Precision.HIGHEST
        )
        results[height] = segment
        settled[height] = segment.astype(jnp.bfloat16)
    return (jnp.stack(solved), jnp.stack(results))


def solution(mesh):
    placed = (
        P(None, "row", None, None),
        P(None, "row", None, None),
        P(None, "row", "col", None, None),
        P(None, "row", "col"),
    )
    return jax.shard_map(
        shards,
        mesh=mesh,
        in_specs=placed,
        out_specs=(P(None, "row", None, None), P(None, "row", None, None)),
        check_vma=False,
    )
```

profile of v0, /device:TPU:0, one launch (start us, length us, event | category | flops | bytes accessed | tf_op | source)
XLA Modules:
  0.0 446.8 jit_solution(956539431709333284)
XLA Ops:
  0.7 1.7 compare_reduce_fusion
  2.3 1.1 bitcast_dynamic-update-slice_fusion.10
  3.5 32.3 %all-gather = bf16[512,128]{1,0:T(8,128)(2,1)S(1)} all-gather(bf16[64,128]{1,0:T(8,128)(2,1)S(1)} %convert_element_type.125), channel_id=2, replica_groups=mesh['row'=8,'col'=4] {'row'}, dimensions={0}, use_global_device_ids=true | all-gather | bytes 147456 | tf_op jit(solution)/shard_map/all_gather | solution.py:47
  35.8 1.0 fusion.24
  36.8 10.1 %psum.105 = bf16[1,64,128]{2,1,0:T(8,128)(2,1)S(1)} all-reduce(bf16[1,64,128]{2,1,0:T(8,128)(2,1)S(1)} %fusion.24), channel_id=1, replica_groups=mesh['row'=8,'col'=4] {'col'}, use_global_device_ids=true, to_apply=%region_0.1 | all-reduce | flops 8192 | bytes 32768 | tf_op jit(solution)/shard_map/psum | solution.py:40
  47.0 1.1 bitcast_dynamic-update-slice_fusion.9
  48.1 1.0 convolution_bitcast_fusion.15
  49.1 0.2 convolution_bitcast_fusion.13
  49.4 0.2 convolution_bitcast_fusion.10
  49.6 0.2 convolution_bitcast_fusion.6
  49.8 30.7 %all-gather.1 = bf16[512,128]{1,0:T(8,128)(2,1)S(1)} all-gather(bf16[64,128]{1,0:T(8,128)(2,1)S(1)} %convert_element_type.130), channel_id=3, replica_groups=mesh['row'=8,'col'=4] {'row'}, dimensions={0}, use_global_device_ids=true | all-gather | bytes 147456 | tf_op jit(solution)/shard_map/all_gather | solution.py:47
  80.7 10.1 %psum.106 = bf16[1,64,128]{2,1,0:T(8,128)(2,1)S(1)} all-reduce(bf16[1,64,128]{2,1,0:T(8,128)(2,1)S(1)} %fusion.23), channel_id=1, replica_groups=mesh['row'=8,'col'=4] {'col'}, use_global_device_ids=true, to_apply=%region_1.2 | all-reduce | flops 8192 | bytes 32768 | tf_op jit(solution)/shard_map/psum | solution.py:40
  91.0 0.2 fusion.11
  91.3 0.2 fusion.8
  91.5 0.5 copy-done.2
  92.0 0.2 bitcast_dynamic-update-slice_fusion.8
  92.2 30.5 %all-gather.2 = bf16[512,128]{1,0:T(8,128)(2,1)S(1)} all-gather(bf16[64,128]{1,0:T(8,128)(2,1)S(1)} %convert_element_type.135), channel_id=4, replica_groups=mesh['row'=8,'col'=4] {'row'}, dimensions={0}, use_global_device_ids=true | all-gather | bytes 147456 | tf_op jit(solution)/shard_map/all_gather | solution.py:47
  123.0 10.1 %psum.107 = bf16[1,64,128]{2,1,0:T(8,128)(2,1)S(1)} all-reduce(bf16[1,64,128]{2,1,0:T(8,128)(2,1)S(1)} %fusion.22), channel_id=1, replica_groups=mesh['row'=8,'col'=4] {'col'}, use_global_device_ids=true, to_apply=%region_2.3 | all-reduce | flops 8192 | bytes 32768 | tf_op jit(solution)/shard_map/psum | solution.py:40
  133.3 0.2 fusion.7
  133.5 0.3 bitcast_dynamic-update-slice_fusion.7
  133.8 30.5 %all-gather.3 = bf16[512,128]{1,0:T(8,128)(2,1)S(1)} all-gather(bf16[64,128]{1,0:T(8,128)(2,1)S(1)} %convert_element_type.140), channel_id=5, replica_groups=mesh['row'=8,'col'=4] {'row'}, dimensions={0}, use_global_device_ids=true | all-gather | bytes 147456 | tf_op jit(solution)/shard_map/all_gather | solution.py:47
  164.5 0.2 fusion.6
  164.8 10.1 %psum.108 = bf16[1,64,128]{2,1,0:T(8,128)(2,1)S(1)} all-reduce(bf16[1,64,128]{2,1,0:T(8,128)(2,1)S(1)} %fusion.21), channel_id=1, replica_groups=mesh['row'=8,'col'=4] {'col'}, use_global_device_ids=true, to_apply=%region_3.4 | all-reduce | flops 8192 | bytes 32768 | tf_op jit(solution)/shard_map/psum | solution.py:40
  174.9 0.2 bitcast_dynamic-update-slice_fusion.6
  175.2 30.5 %all-gather.4 = bf16[512,128]{1,0:T(8,128)(2,1)S(1)} all-gather(bf16[64,128]{1,0:T(8,128)(2,1)S(1)} %convert_element_type.145), channel_id=6, replica_groups=mesh['row'=8,'col'=4] {'row'}, dimensions={0}, use_global_device_ids=true | all-gather | bytes 147456 | tf_op jit(solution)/shard_map/all_gather | solution.py:47
  205.9 10.1 %psum.109 = bf16[1,64,128]{2,1,0:T(8,128)(2,1)S(1)} all-reduce(bf16[1,64,128]{2,1,0:T(8,128)(2,1)S(1)} %fusion.20), channel_id=1, replica_groups=mesh['row'=8,'col'=4] {'col'}, use_global_device_ids=true, to_apply=%region_4.5 | all-reduce | flops 8192 | bytes 32768 | tf_op jit(solution)/shard_map/psum | solution.py:40
  216.0 0.2 bitcast_dynamic-update-slice_fusion.5
  216.7 37.5 %psum.110 = bf16[2,64,128]{2,1,0:T(8,128)(2,1)S(1)} all-reduce(f32[2,64,128]{2,1,0:T(8,128)S(1)} %convolution_bitcast_fusion), channel_id=1, replica_groups=mesh['row'=8,'col'=4] {'row'}, use_global_device_ids=true, to_apply=%region_5.6 | all-reduce | flops 16384 | bytes 98304 | tf_op jit(solution)/shard_map/psum | solution.py:64
  254.2 10.1 %psum.111 = bf16[1,64,128]{2,1,0:T(8,128)(2,1)S(1)} all-reduce(bf16[1,64,128]{2,1,0:T(8,128)(2,1)S(1)} %fusion.221), channel_id=1, replica_groups=mesh['row'=8,'col'=4] {'col'}, use_global_device_ids=true, to_apply=%region_6.7 | all-reduce | flops 8192 | bytes 32768 | tf_op jit(solution)/shard_map/psum | solution.py:9
  264.7 0.2 fusion.3
  264.9 33.4 %psum.112 = bf16[2,64,128]{2,1,0:T(8,128)(2,1)S(1)} all-reduce(f32[2,64,128]{2,1,0:T(8,128)S(1)} %fusion.3), channel_id=1, replica_groups=mesh['row'=8,'col'=4] {'row'}, use_global_device_ids=true, to_apply=%region_7.8 | all-reduce | flops 16384 | bytes 98304 | tf_op jit(solution)/shard_map/psum | solution.py:64
  298.3 10.1 %psum.113 = bf16[1,64,128]{2,1,0:T(8,128)(2,1)S(1)} all-reduce(bf16[1,64,128]{2,1,0:T(8,128)(2,1)S(1)} %fusion.222), channel_id=1, replica_groups=mesh['row'=8,'col'=4] {'col'}, use_global_device_ids=true, to_apply=%region_8.9 | all-reduce | flops 8192 | bytes 32768 | tf_op jit(solution)/shard_map/psum | solution.py:9
  308.8 0.2 convolution_add_fusion.8
  309.0 0.2 fusion.2
  309.2 35.3 %psum.114 = bf16[2,64,128]{2,1,0:T(8,128)(2,1)S(1)} all-reduce(f32[2,64,128]{2,1,0:T(8,128)S(1)} %fusion.2), channel_id=1, replica_groups=mesh['row'=8,'col'=4] {'row'}, use_global_device_ids=true, to_apply=%region_9.10 | all-reduce | flops 16384 | bytes 98304 | tf_op jit(solution)/shard_map/psum | solution.py:64
  344.6 10.1 %psum.115 = bf16[1,64,128]{2,1,0:T(8,128)(2,1)S(1)} all-reduce(bf16[1,64,128]{2,1,0:T(8,128)(2,1)S(1)} %fusion.223), channel_id=1, replica_groups=mesh['row'=8,'col'=4] {'col'}, use_global_device_ids=true, to_apply=%region_10.11 | all-reduce | flops 8192 | bytes 32768 | tf_op jit(solution)/shard_map/psum | solution.py:9
  355.1 0.2 convolution_add_fusion.6
  355.3 0.2 convolution_add_fusion.5
  355.5 0.2 fusion.1
  355.7 33.4 %psum.116 = bf16[2,64,128]{2,1,0:T(8,128)(2,1)S(1)} all-reduce(f32[2,64,128]{2,1,0:T(8,128)S(1)} %fusion.1), channel_id=1, replica_groups=mesh['row'=8,'col'=4] {'row'}, use_global_device_ids=true, to_apply=%region_11.12 | all-reduce | flops 16384 | bytes 98304 | tf_op jit(solution)/shard_map/psum | solution.py:64
  389.1 10.1 %psum.117 = bf16[1,64,128]{2,1,0:T(8,128)(2,1)S(1)} all-reduce(bf16[1,64,128]{2,1,0:T(8,128)(2,1)S(1)} %fusion.224), channel_id=1, replica_groups=mesh['row'=8,'col'=4] {'col'}, use_global_device_ids=true, to_apply=%region_12.13 | all-reduce | flops 8192 | bytes 32768 | tf_op jit(solution)/shard_map/psum | solution.py:9
  399.6 0.2 convolution_add_fusion.3
  399.8 0.2 convolution_add_fusion.2
  400.0 0.2 convolution_add_fusion.1
  400.2 0.2 fusion
  400.4 35.3 %psum.118 = bf16[2,64,128]{2,1,0:T(8,128)(2,1)S(1)} all-reduce(f32[2,64,128]{2,1,0:T(8,128)S(1)} %fusion), channel_id=1, replica_groups=mesh['row'=8,'col'=4] {'row'}, use_global_device_ids=true, to_apply=%region_13.14 | all-reduce | flops 16384 | bytes 98304 | tf_op jit(solution)/shard_map/psum | solution.py:64
  435.8 10.1 %psum.119 = bf16[1,64,128]{2,1,0:T(8,128)(2,1)S(1)} all-reduce(bf16[1,64,128]{2,1,0:T(8,128)(2,1)S(1)} %fusion.225), channel_id=1, replica_groups=mesh['row'=8,'col'=4] {'col'}, use_global_device_ids=true, to_apply=%region_14.15 | all-reduce | flops 8192 | bytes 32768 | tf_op jit(solution)/shard_map/psum | solution.py:9
  446.2 0.7 copy-done.4
  (40 shorter events, 3.4 us)
Async XLA Ops:
  0.6 48.5 %copy-start = (bf16[15,1,2,128,128]{4,3,2,1,0:T(8,128)(2,1)S(1)}, bf16[15,1,2,128,128]{4,3,2,1,0:T(8,128)(2,1)}, u32[]{:S(2)}) copy-start(bf16[15,1,2,128,128]{4,3,2,1,0:T(8,128)(2,1)} %param.6) | copy-start | bytes 2949124
  49.8 41.7 %copy-start.1 = (f32[6,1,128,128]{3,2,1,0:T(8,128)S(1)}, f32[6,1,128,128]{3,2,1,0:T(8,128)}, u32[]{:S(2)}) copy-start(f32[6,1,128,128]{3,2,1,0:T(8,128)} %param.5) | copy-start | bytes 1179652
  91.0 1.0 copy-start.2
  216.3 37.9 %copy-start.3 = (f32[6,1,64,128]{3,2,1,0:T(8,128)}, f32[6,1,64,128]{3,2,1,0:T(8,128)S(1)}, u32[]{:S(2)}) copy-start(f32[6,1,64,128]{3,2,1,0:T(8,128)S(1)} %get-tuple-element.27) | copy-start | bytes 589828
  446.1 0.7 copy-start.4
where the time goes:
time: 448 us; the launch traced here: 447 us
  blocking collectives  431 us (96%)
  matrix products  12.2 us (3%)
    psum x5, blocking collectives, shards(): summed = lax.psum(partial_value, 'row')  175 us
    all_gather x5, blocking collectives, shards(): lax.all_gather(segment.astype(jnp.bfloat16), 'row', axis=0, tiled=True)  155 us
    psum x5, blocking collectives, shards(): lax.psum(partial_value.astype(jnp.bfloat16), 'col').astype(jnp.float32)  50.7 us
    psum x5, blocking collectives, spread(): return lax.psum(block, axis)  50.6 us

commit v1 on v0

--- a/solution.py
+++ b/solution.py
@@ -6,7 +6,7 @@
 
 def spread(block, axis, holder):
     block = jnp.where(lax.axis_index(axis) == holder, block, jnp.zeros_like(block))
-    return lax.psum(block, axis)
+    return jnp.sum(lax.all_gather(block, axis), axis=0)
 
 
 def pair_number(higher, lower_level):

time: 448 us -> 423 us (0.944)
  blocking collectives: 431 us -> 406 us
    psum x5 -> x0, blocking collectives: 50.6 us -> none  [spread(): return lax.psum(block, axis)]
    all_gather x0 -> x5, blocking collectives: none -> 26.2 us  [spread(): return jnp.sum(lax.all_gather(block, axis), axis=0)]
where the time goes in v1:
time: 423 us; the launch traced here: 422 us
  blocking collectives  406 us (96%)
  matrix products  12.2 us (3%)
    psum x5, blocking collectives, shards(): summed = lax.psum(partial_value, 'row')  175 us
    all_gather x5, blocking collectives, shards(): lax.all_gather(segment.astype(jnp.bfloat16), 'row', axis=0, tiled=True)  155 us
    psum x5, blocking collectives, shards(): lax.psum(partial_value.astype(jnp.bfloat16), 'col').astype(jnp.float32)  50.7 us
    all_gather x5, blocking collectives, spread(): return jnp.sum(lax.all_gather(block, axis), axis=0)  26.2 us

profile of v1, /device:TPU:0, one launch (start us, length us, event | category | flops | bytes accessed | tf_op | source)
XLA Modules:
  0.0 422.5 jit_solution(4892088226130643865)
XLA Ops:
  0.7 1.7 compare_reduce_fusion
  2.3 1.1 bitcast_dynamic-update-slice_fusion.10
  3.5 32.3 %all-gather = bf16[512,128]{1,0:T(8,128)(2,1)S(1)} all-gather(bf16[64,128]{1,0:T(8,128)(2,1)S(1)} %convert_element_type.140), channel_id=2, replica_groups=mesh['row'=8,'col'=4] {'row'}, dimensions={0}, use_global_device_ids=true | all-gather | bytes 147456 | tf_op jit(solution)/shard_map/all_gather | solution.py:47
  35.8 1.0 fusion.24
  36.8 10.1 %psum.70 = bf16[1,64,128]{2,1,0:T(8,128)(2,1)S(1)} all-reduce(bf16[1,64,128]{2,1,0:T(8,128)(2,1)S(1)} %fusion.24), channel_id=1, replica_groups=mesh['row'=8,'col'=4] {'col'}, use_global_device_ids=true, to_apply=%region_0.1 | all-reduce | flops 8192 | bytes 32768 | tf_op jit(solution)/shard_map/psum | solution.py:40
  47.0 1.1 bitcast_dynamic-update-slice_fusion.9
  48.1 1.0 convolution_bitcast_fusion.15
  49.1 0.2 convolution_bitcast_fusion.13
  49.4 0.2 convolution_bitcast_fusion.10
  49.6 0.2 convolution_bitcast_fusion.6
  49.8 30.7 %all-gather.1 = bf16[512,128]{1,0:T(8,128)(2,1)S(1)} all-gather(bf16[64,128]{1,0:T(8,128)(2,1)S(1)} %convert_element_type.145), channel_id=3, replica_groups=mesh['row'=8,'col'=4] {'row'}, dimensions={0}, use_global_device_ids=true | all-gather | bytes 147456 | tf_op jit(solution)/shard_map/all_gather | solution.py:47
  80.7 10.1 %psum.71 = bf16[1,64,128]{2,1,0:T(8,128)(2,1)S(1)} all-reduce(bf16[1,64,128]{2,1,0:T(8,128)(2,1)S(1)} %fusion.23), channel_id=1, replica_groups=mesh['row'=8,'col'=4] {'col'}, use_global_device_ids=true, to_apply=%region_1.2 | all-reduce | flops 8192 | bytes 32768 | tf_op jit(solution)/shard_map/psum | solution.py:40
  91.0 0.2 fusion.11
  91.3 0.2 fusion.8
  91.5 0.5 copy-done.2
  92.0 0.2 bitcast_dynamic-update-slice_fusion.8
  92.2 30.5 %all-gather.2 = bf16[512,128]{1,0:T(8,128)(2,1)S(1)} all-gather(bf16[64,128]{1,0:T(8,128)(2,1)S(1)} %convert_element_type.150), channel_id=4, replica_groups=mesh['row'=8,'col'=4] {'row'}, dimensions={0}, use_global_device_ids=true | all-gather | bytes 147456 | tf_op jit(solution)/shard_map/all_gather | solution.py:47
  123.0 10.1 %psum.72 = bf16[1,64,128]{2,1,0:T(8,128)(2,1)S(1)} all-reduce(bf16[1,64,128]{2,1,0:T(8,128)(2,1)S(1)} %fusion.22), channel_id=1, replica_groups=mesh['row'=8,'col'=4] {'col'}, use_global_device_ids=true, to_apply=%region_2.3 | all-reduce | flops 8192 | bytes 32768 | tf_op jit(solution)/shard_map/psum | solution.py:40
  133.3 0.2 fusion.7
  133.5 0.3 bitcast_dynamic-update-slice_fusion.7
  133.8 30.5 %all-gather.3 = bf16[512,128]{1,0:T(8,128)(2,1)S(1)} all-gather(bf16[64,128]{1,0:T(8,128)(2,1)S(1)} %convert_element_type.155), channel_id=5, replica_groups=mesh['row'=8,'col'=4] {'row'}, dimensions={0}, use_global_device_ids=true | all-gather | bytes 147456 | tf_op jit(solution)/shard_map/all_gather | solution.py:47
  164.5 0.2 fusion.6
  164.8 10.1 %psum.73 = bf16[1,64,128]{2,1,0:T(8,128)(2,1)S(1)} all-reduce(bf16[1,64,128]{2,1,0:T(8,128)(2,1)S(1)} %fusion.21), channel_id=1, replica_groups=mesh['row'=8,'col'=4] {'col'}, use_global_device_ids=true, to_apply=%region_3.4 | all-reduce | flops 8192 | bytes 32768 | tf_op jit(solution)/shard_map/psum | solution.py:40
  174.9 0.2 bitcast_dynamic-update-slice_fusion.6
  175.2 30.5 %all-gather.4 = bf16[512,128]{1,0:T(8,128)(2,1)S(1)} all-gather(bf16[64,128]{1,0:T(8,128)(2,1)S(1)} %convert_element_type.160), channel_id=6, replica_groups=mesh['row'=8,'col'=4] {'row'}, dimensions={0}, use_global_device_ids=true | all-gather | bytes 147456 | tf_op jit(solution)/shard_map/all_gather | solution.py:47
  205.9 10.1 %psum.74 = bf16[1,64,128]{2,1,0:T(8,128)(2,1)S(1)} all-reduce(bf16[1,64,128]{2,1,0:T(8,128)(2,1)S(1)} %fusion.20), channel_id=1, replica_groups=mesh['row'=8,'col'=4] {'col'}, use_global_device_ids=true, to_apply=%region_4.5 | all-reduce | flops 8192 | bytes 32768 | tf_op jit(solution)/shard_map/psum | solution.py:40
  216.0 0.2 bitcast_dynamic-update-slice_fusion.5
  216.7 37.5 %psum.75 = bf16[2,64,128]{2,1,0:T(8,128)(2,1)S(1)} all-reduce(f32[2,64,128]{2,1,0:T(8,128)S(1)} %convolution_bitcast_fusion), channel_id=1, replica_groups=mesh['row'=8,'col'=4] {'row'}, use_global_device_ids=true, to_apply=%region_5.6 | all-reduce | flops 16384 | bytes 98304 | tf_op jit(solution)/shard_map/psum | solution.py:64
  254.2 5.2 %all-gather.5 = bf16[4,64,128]{2,1,0:T(8,128)(2,1)S(1)} all-gather(bf16[1,64,128]{2,1,0:T(8,128)(2,1)S(1)} %fusion.221), channel_id=7, replica_groups=mesh['row'=8,'col'=4] {'col'}, dimensions={0}, use_global_device_ids=true | all-gather | bytes 81920 | tf_op jit(solution)/shard_map/all_gather | solution.py:9
  259.8 0.2 fusion.3
  260.0 33.4 %psum.76 = bf16[2,64,128]{2,1,0:T(8,128)(2,1)S(1)} all-reduce(f32[2,64,128]{2,1,0:T(8,128)S(1)} %fusion.3), channel_id=1, replica_groups=mesh['row'=8,'col'=4] {'row'}, use_global_device_ids=true, to_apply=%region_7.8 | all-reduce | flops 16384 | bytes 98304 | tf_op jit(solution)/shard_map/psum | solution.py:64
  293.4 5.2 %all-gather.6 = bf16[4,64,128]{2,1,0:T(8,128)(2,1)S(1)} all-gather(bf16[1,64,128]{2,1,0:T(8,128)(2,1)S(1)} %fusion.222), channel_id=8, replica_groups=mesh['row'=8,'col'=4] {'col'}, dimensions={0}, use_global_device_ids=true | all-gather | bytes 81920 | tf_op jit(solution)/shard_map/all_gather | solution.py:9
  299.1 0.2 convolution_add_fusion.8
  299.3 0.2 fusion.2
  299.5 35.3 %psum.77 = bf16[2,64,128]{2,1,0:T(8,128)(2,1)S(1)} all-reduce(f32[2,64,128]{2,1,0:T(8,128)S(1)} %fusion.2), channel_id=1, replica_groups=mesh['row'=8,'col'=4] {'row'}, use_global_device_ids=true, to_apply=%region_9.10 | all-reduce | flops 16384 | bytes 98304 | tf_op jit(solution)/shard_map/psum | solution.py:64
  334.8 5.2 %all-gather.7 = bf16[4,64,128]{2,1,0:T(8,128)(2,1)S(1)} all-gather(bf16[1,64,128]{2,1,0:T(8,128)(2,1)S(1)} %fusion.223), channel_id=9, replica_groups=mesh['row'=8,'col'=4] {'col'}, dimensions={0}, use_global_device_ids=true | all-gather | bytes 81920 | tf_op jit(solution)/shard_map/all_gather | solution.py:9
  340.5 0.2 convolution_add_fusion.6
  340.7 0.2 convolution_add_fusion.5
  340.9 0.2 fusion.1
  341.1 33.4 %psum.78 = bf16[2,64,128]{2,1,0:T(8,128)(2,1)S(1)} all-reduce(f32[2,64,128]{2,1,0:T(8,128)S(1)} %fusion.1), channel_id=1, replica_groups=mesh['row'=8,'col'=4] {'row'}, use_global_device_ids=true, to_apply=%region_11.12 | all-reduce | flops 16384 | bytes 98304 | tf_op jit(solution)/shard_map/psum | solution.py:64
  374.5 5.2 %all-gather.8 = bf16[4,64,128]{2,1,0:T(8,128)(2,1)S(1)} all-gather(bf16[1,64,128]{2,1,0:T(8,128)(2,1)S(1)} %fusion.224), channel_id=10, replica_groups=mesh['row'=8,'col'=4] {'col'}, dimensions={0}, use_global_device_ids=true | all-gather | bytes 81920 | tf_op jit(solution)/shard_map/all_gather | solution.py:9
  380.1 0.2 convolution_add_fusion.3
  380.3 0.2 convolution_add_fusion.2
  380.5 0.2 convolution_add_fusion.1
  380.8 0.2 fusion
  381.0 35.3 %psum.79 = bf16[2,64,128]{2,1,0:T(8,128)(2,1)S(1)} all-reduce(f32[2,64,128]{2,1,0:T(8,128)S(1)} %fusion), channel_id=1, replica_groups=mesh['row'=8,'col'=4] {'row'}, use_global_device_ids=true, to_apply=%region_13.14 | all-reduce | flops 16384 | bytes 98304 | tf_op jit(solution)/shard_map/psum | solution.py:64
  416.3 5.2 %all-gather.9 = bf16[4,64,128]{2,1,0:T(8,128)(2,1)S(1)} all-gather(bf16[1,64,128]{2,1,0:T(8,128)(2,1)S(1)} %fusion.225), channel_id=11, replica_groups=mesh['row'=8,'col'=4] {'col'}, dimensions={0}, use_global_device_ids=true | all-gather | bytes 81920 | tf_op jit(solution)/shard_map/all_gather | solution.py:9
  421.8 0.7 copy-done.4
  (45 shorter events, 3.5 us)
Async XLA Ops:
  0.6 48.5 %copy-start = (bf16[15,1,2,128,128]{4,3,2,1,0:T(8,128)(2,1)S(1)}, bf16[15,1,2,128,128]{4,3,2,1,0:T(8,128)(2,1)}, u32[]{:S(2)}) copy-start(bf16[15,1,2,128,128]{4,3,2,1,0:T(8,128)(2,1)} %param.6) | copy-start | bytes 2949124
  49.8 41.7 %copy-start.1 = (f32[6,1,128,128]{3,2,1,0:T(8,128)S(1)}, f32[6,1,128,128]{3,2,1,0:T(8,128)}, u32[]{:S(2)}) copy-start(f32[6,1,128,128]{3,2,1,0:T(8,128)} %param.5) | copy-start | bytes 1179652
  91.0 1.0 copy-start.2
  216.3 37.9 %copy-start.3 = (f32[6,1,64,128]{3,2,1,0:T(8,128)}, f32[6,1,64,128]{3,2,1,0:T(8,128)S(1)}, u32[]{:S(2)}) copy-start(f32[6,1,64,128]{3,2,1,0:T(8,128)S(1)} %get-tuple-element.27) | copy-start | bytes 589828
  421.8 0.7 copy-start.4
